TPU v7x, 32 devices: a whole 2x2x4 slice. The times are simulated.
32 devices in a mesh: dp: 8 (over y, x, core), tensor: 4 (over z).
Axes of the slice: x: 2, y: 2, z: 4, core: 2. Of those that a mesh axis runs over, the one named last changes fastest.
Arguments:
- tokens: bfloat16 [16, 1024, 1024], P('dp', 'tensor'), may hold values from -6 to 6
- segments: int32 [16, 1024], P('dp'), may hold values from 0 to 3, as said below
- qkv_weight: bfloat16 [3, 1024, 1024], P(None, None, 'tensor'), may hold values from -0.1875 to 0.1875
- qkv_bias: float32 [3, 1024], P(None, 'tensor'), may hold values from -1.5 to 1.5
- out_weight: bfloat16 [1024, 1024], P('tensor'), may hold values from -0.75 to 0.75
- out_bias: float32 [1024], replicated, may hold values from -1.5 to 1.5
- gain_one: float32 [1024], replicated, may hold values from 0.5 to 1.5
- shift_one: float32 [1024], replicated, may hold values from -1.5 to 1.5
- up_weight: bfloat16 [1024, 4096], P(None, 'tensor'), may hold values from -0.1875 to 0.1875
- up_bias: float32 [4096], P('tensor'), may hold values from -1.5 to 1.5
- down_weight: bfloat16 [4096, 1024], P('tensor'), may hold values from -0.1875 to 0.1875
- down_bias: float32 [1024], replicated, may hold values from -1.5 to 1.5
- gain_two: float32 [1024], replicated, may hold values from 0.5 to 1.5
- shift_two: float32 [1024], replicated, may hold values from -1.5 to 1.5
- proj_weight: bfloat16 [1024, 288], replicated, may hold values from -0.1875 to 0.1875
- out_grad: bfloat16 [16, 1024, 1024], P('dp', 'tensor'), may hold values from -6 to 6
- embed_grad: bfloat16 [16, 1024, 288], P('dp', 'tensor'), may hold values from -6 to 6
Outputs:
- layer_out: bfloat16 [16, 1024, 1024], P('dp', 'tensor')
- embeddings: bfloat16 [16, 1024, 288], P('dp', 'tensor')
- tokens_grad: float32 [16, 1024, 1024], P('dp', 'tensor')
- qkv_weight_grad: float32 [3, 1024, 1024], P(None, None, 'tensor')
- qkv_bias_grad: float32 [3, 1024], P(None, 'tensor')
- out_weight_grad: float32 [1024, 1024], P('tensor')
- out_bias_grad: float32 [1024], replicated
- gain_one_grad: float32 [1024], replicated
- shift_one_grad: float32 [1024], replicated
- up_weight_grad: float32 [1024, 4096], P(None, 'tensor')
- up_bias_grad: float32 [4096], P('tensor')
- down_weight_grad: float32 [4096, 1024], P('tensor')
- down_bias_grad: float32 [1024], replicated
- gain_two_grad: float32 [1024], replicated
- shift_two_grad: float32 [1024], replicated
- proj_weight_grad: float32 [1024, 288], replicated
Inputs may be any that keep to these rules, and one draw needn't show every extreme that they name: `segments`: segment numbers never fall along a sequence; every sequence holds 4 documents, each of at least 200 tokens, and in every sequence some document has exactly 200.
All inputs are finite; a program needn't handle non-finite values.
Results may differ from a plain program's by a relative error of at most 0.018.
Values may be sent and summed in bfloat16 or wider, within the bound.
A program may use at most 192 MiB of HBM per device.

v0:
```python
import math
import jax
import jax.numpy as jnp
from jax import lax
from jax.sharding import Mesh
from jax.sharding import PartitionSpec as P

HEAD_DIM = 64
eps = 1e-05
DP = ("xb", "x", "yb", "y", "core")
CELL = ("x", "y", "core")
ALL = DP + ("z",)
f32 = jnp.float32
bf16 = jnp.bfloat16


def doc_positions(segment_rows):
    length = segment_rows.shape[-1]
    row_index = jnp.broadcast_to(jnp.arange(length, dtype=jnp.int32), segment_rows.shape)
    change = jnp.concatenate(
        [
            jnp.ones(segment_rows.shape[:-1] + (1,), jnp.bool_),
            segment_rows[..., 1:] != segment_rows[..., :-1],
        ],
        axis=-1,
    )
    doc_start = lax.cummax(
        jnp.where(change, row_index, jnp.zeros_like(row_index)), axis=segment_rows.ndim - 1
    )
    return row_index - doc_start


def rotary_tables(positions, head_dim):
    half_dim = head_dim // 2
    exponent = jnp.arange(half_dim, dtype=f32) * (2.0 / head_dim)
    frequency = jnp.exp(-exponent * math.log(10000.0))
    angles = positions.astype(f32)[..., None] * frequency
    angles = jnp.concatenate([angles, angles], axis=-1)
    return (jnp.cos(angles), jnp.sin(angles))


def rotate(field, cosine, sine):
    half_dim = field.shape[-1] // 2
    rotated = jnp.concatenate([-field[..., half_dim:], field[..., :half_dim]], axis=-1)
    return field * cosine + rotated * sine


def rotate_back(field, cosine, sine):
    half_dim = field.shape[-1] // 2
    rotated = jnp.concatenate([-field[..., half_dim:], field[..., :half_dim]], axis=-1)
    return field * cosine - rotated * sine


def norm_forward(field, gain, shift):
    row_mean = jnp.mean(field, axis=-1, keepdims=True)
    centred = field - row_mean
    variance = jnp.mean(centred * centred, axis=-1, keepdims=True)
    inv_std = lax.rsqrt(variance + eps)
    scaled = centred * inv_std
    return (scaled * gain + shift, scaled, inv_std)


def norm_backward(upstream, scaled, inv_std, gain):
    grad_scaled = upstream * gain
    grad_input = inv_std * (
        grad_scaled
        - jnp.mean(grad_scaled, axis=-1, keepdims=True)
        - scaled * jnp.mean(grad_scaled * scaled, axis=-1, keepdims=True)
    )
    return (grad_input, jnp.sum(upstream * scaled, axis=0), jnp.sum(upstream, axis=0))


def masked_scores(queries, keys, seg_row):
    scores = jnp.einsum("hqd,hkd->hqk", queries, keys, preferred_element_type=f32)
    same_doc = seg_row[:, None] == seg_row[None, :]
    return jnp.where(same_doc[None], scores, -1000000000.0)


def attend(inputs):
    queries, keys, values_low, seg_row = inputs
    scores = masked_scores(queries, keys, seg_row)
    row_peak = jnp.max(scores, axis=-1, keepdims=True)
    shifted = jnp.exp(scores - row_peak)
    row_total = jnp.sum(shifted, axis=-1, keepdims=True)
    probs = (shifted / row_total).astype(bf16)
    mixed_heads = jnp.einsum("hqk,hkd->hqd", probs, values_low, preferred_element_type=f32)
    return (mixed_heads, row_peak + jnp.log(row_total))


def attend_back(inputs):
    queries, keys, values_low, seg_row, log_total, grad_mixed = inputs
    scores = masked_scores(queries, keys, seg_row)
    probs = jnp.exp(scores - log_total)
    grad_values = jnp.einsum(
        "hqk,hqd->hkd", probs.astype(bf16), grad_mixed, preferred_element_type=f32
    )
    grad_probs = jnp.einsum("hqd,hkd->hqk", grad_mixed, values_low, preferred_element_type=f32)
    row_inner = jnp.sum(probs * grad_probs, axis=-1, keepdims=True)
    grad_scores = (probs * (grad_probs - row_inner)).astype(bf16)
    grad_queries = jnp.einsum("hqk,hkd->hqd", grad_scores, keys, preferred_element_type=f32)
    grad_keys = jnp.einsum("hqk,hqd->hkd", grad_scores, queries, preferred_element_type=f32)
    return (grad_queries, grad_keys, grad_values)


def piece_of(shard):
    rows = shard.shape[0] // 8
    return lax.dynamic_slice_in_dim(shard, lax.axis_index(CELL) * rows, rows, 0)


def gather_all(shard, zsize):
    whole = lax.all_gather(piece_of(shard), ("z",) + CELL, axis=0, tiled=True)
    return whole.reshape((zsize,) + shard.shape)


def reduce_all(partial):
    rows = partial.shape[0] * partial.shape[1]
    piece = lax.psum_scatter(
        partial.reshape(rows, partial.shape[2]), ("z",) + CELL, scatter_dimension=0, tiled=True
    )
    return lax.all_gather(piece, CELL, axis=0, tiled=True)


def per_device(
    blocks,
    tokens,
    segments,
    qkv_weight,
    qkv_bias,
    out_weight,
    out_bias,
    gain_one,
    shift_one,
    up_weight,
    up_bias,
    down_weight,
    down_bias,
    gain_two,
    shift_two,
    proj_weight,
    out_grad,
    embed_grad,
):
    groups, local_rows, model_width = tokens.shape
    length = segments.shape[1]
    zsize = length // local_rows
    heads_here = qkv_weight.shape[2] // HEAD_DIM
    head_cols = qkv_weight.shape[2]
    units_here = up_weight.shape[1]
    rows = groups * local_rows
    zi = lax.axis_index("z")
    q_scale = HEAD_DIM ** (-0.5)
    cosine, sine = rotary_tables(doc_positions(segments), HEAD_DIM)
    cosine = cosine[:, None]
    sine = sine[:, None]

    def split_heads(field):
        return field.reshape(groups, length, heads_here, HEAD_DIM).transpose(0, 2, 1, 3)

    def join_heads(field):
        return field.transpose(0, 2, 1, 3).reshape(groups, length, head_cols)

    whole_tokens = lax.all_gather(tokens, "z", axis=1, tiled=True)
    out_all = gather_all(out_weight, zsize).reshape(model_width, model_width)
    up_all = gather_all(up_weight, zsize)
    down_all = gather_all(down_weight, zsize)
    full_up_bias = lax.all_gather(up_bias, "z", axis=0, tiled=False)
    projected = jnp.einsum("gld,cde->cgle", whole_tokens, qkv_weight, preferred_element_type=f32)
    projected = projected + qkv_bias[:, None, None, :]
    queries = (rotate(split_heads(projected[0]), cosine, sine) * q_scale).astype(bf16)
    keys = rotate(split_heads(projected[1]), cosine, sine).astype(bf16)
    values_low = split_heads(projected[2]).astype(bf16)
    got = [attend((queries[g], keys[g], values_low[g], segments[g])) for g in range(groups)]
    log_total = [g[1] for g in got]
    mixed = join_heads(jnp.stack([g[0] for g in got])).astype(bf16)
    mixed = lax.all_to_all(mixed, "z", split_axis=1, concat_axis=2, tiled=True).reshape(
        rows, model_width
    )
    first_sum = tokens.reshape(rows, model_width).astype(f32) + (
        jnp.dot(mixed, out_all, preferred_element_type=f32) + out_bias
    )
    normed, scaled_one, inv_one = norm_forward(first_sum, gain_one, shift_one)
    normed_low = normed.astype(bf16)
    hidden = jnp.einsum("nd,zdf->znf", normed_low, up_all, preferred_element_type=f32)
    hidden = hidden + full_up_bias[:, None, :]
    active, gelu_pull = jax.vjp(lambda field: jax.nn.gelu(field, approximate=False), hidden)
    active = active.astype(bf16)
    ffn = jnp.einsum("znf,zfd->nd", active, down_all, preferred_element_type=f32)
    second_sum = normed + (ffn + down_bias)
    result, scaled_two, inv_two = norm_forward(second_sum, gain_two, shift_two)
    result_low = result.astype(bf16)
    embedded = jnp.dot(result_low, proj_weight, preferred_element_type=f32).astype(bf16)
    embed_rows = embed_grad.reshape(rows, -1)
    grad_result = out_grad.reshape(rows, model_width).astype(f32) + jnp.einsum(
        "np,dp->nd", embed_rows, proj_weight, preferred_element_type=f32
    )
    proj_grad = jnp.einsum("nd,np->dp", result_low, embed_rows, preferred_element_type=f32)
    grad_second, gain_two_grad, shift_two_grad = norm_backward(
        grad_result, scaled_two, inv_two, gain_two
    )
    second_low = grad_second.astype(bf16)
    down_bias_grad = jnp.sum(second_low.astype(f32), axis=0)
    down_grad = jnp.einsum("znf,nd->zfd", active, second_low, preferred_element_type=f32).astype(
        bf16
    )
    grad_active = jnp.einsum("nd,zfd->znf", second_low, down_all, preferred_element_type=f32)
    grad_hidden = gelu_pull(grad_active)[0].astype(bf16)
    up_bias_grad = jnp.sum(grad_hidden.astype(f32), axis=1)
    up_grad = jnp.einsum("nd,znf->zdf", normed_low, grad_hidden, preferred_element_type=f32).astype(
        bf16
    )
    grad_normed = grad_second + jnp.einsum(
        "znf,zdf->nd", grad_hidden, up_all, preferred_element_type=f32
    )
    grad_first, gain_one_grad, shift_one_grad = norm_backward(
        grad_normed, scaled_one, inv_one, gain_one
    )
    first_low = grad_first.astype(bf16)
    out_bias_grad = jnp.sum(first_low.astype(f32), axis=0)
    out_grad_w = jnp.einsum("nh,nd->hd", mixed, first_low, preferred_element_type=f32).astype(bf16)
    grad_mixed = jnp.einsum("nd,hd->nh", first_low, out_all, preferred_element_type=f32).astype(
        bf16
    )
    grad_mixed = grad_mixed.reshape(groups, local_rows, model_width)
    grad_mixed = lax.all_to_all(grad_mixed, "z", split_axis=2, concat_axis=1, tiled=True)
    grad_mixed = split_heads(grad_mixed)
    back = [
        attend_back((queries[g], keys[g], values_low[g], segments[g], log_total[g], grad_mixed[g]))
        for g in range(groups)
    ]
    grad_queries = rotate_back(jnp.stack([b[0] for b in back]) * q_scale, cosine, sine)
    grad_keys = rotate_back(jnp.stack([b[1] for b in back]), cosine, sine)
    grad_values = jnp.stack([b[2] for b in back])
    grad_qkv = jnp.stack(
        [join_heads(grad_queries), join_heads(grad_keys), join_heads(grad_values)]
    ).astype(bf16)
    qkv_bias_grad = jnp.sum(grad_qkv.astype(f32), axis=(1, 2))
    qkv_weight_grad = jnp.einsum(
        "gld,cgle->cde", whole_tokens, grad_qkv, preferred_element_type=f32
    )
    input_back = jnp.einsum(
        "cgle,cde->gld", grad_qkv, qkv_weight, preferred_element_type=f32
    ).astype(bf16)
    input_back = lax.psum_scatter(input_back, "z", scatter_dimension=1, tiled=True)
    tokens_grad = grad_first.reshape(groups, local_rows, model_width) + input_back.astype(f32)
    qkv_weight_grad = lax.psum(qkv_weight_grad.astype(bf16), DP).astype(f32)
    down_grad = reduce_all(down_grad)
    up_grad = reduce_all(up_grad)
    out_grad_w = reduce_all(out_grad_w.reshape(zsize, head_cols, model_width))
    if blocks > 1:
        down_grad, up_grad, out_grad_w = lax.psum((down_grad, up_grad, out_grad_w), ("xb", "yb"))
    small = jnp.concatenate(
        [
            out_bias_grad,
            gain_one_grad,
            shift_one_grad,
            down_bias_grad,
            gain_two_grad,
            shift_two_grad,
            up_bias_grad.reshape(-1),
            lax.dynamic_update_slice(
                jnp.zeros((zsize, 3 * head_cols), f32), qkv_bias_grad.reshape(1, -1), (zi, 0)
            ).reshape(-1),
        ]
    )
    small = lax.psum(small, ALL)
    proj_grad = lax.psum(proj_grad, ALL)
    base = 6 * model_width
    vec = [small[i * model_width : (i + 1) * model_width] for i in range(6)]
    up_bias_grad = lax.dynamic_slice(small, (base + zi * units_here,), (units_here,))
    qkv_bias_grad = lax.dynamic_slice(
        small, (base + zsize * units_here + zi * 3 * head_cols,), (3 * head_cols,)
    ).reshape(3, head_cols)
    shape3 = (groups, local_rows, model_width)
    return (
        result_low.reshape(shape3),
        embedded.reshape(groups, local_rows, -1),
        tokens_grad,
        qkv_weight_grad,
        qkv_bias_grad,
        out_grad_w.astype(f32),
        vec[0],
        vec[1],
        vec[2],
        up_grad.astype(f32),
        up_bias_grad,
        down_grad.astype(f32),
        vec[3],
        vec[4],
        vec[5],
        proj_grad,
    )


def solution(mesh):
    dp_size, zsize = (mesh.shape["dp"], mesh.shape["tensor"])
    side = math.isqrt(dp_size // 2) // 2
    cut = Mesh(mesh.devices.reshape(side, 2, side, 2, 2, zsize), DP + ("z",))
    rows3 = P(DP, "z", None)
    in_specs = (
        rows3,
        P(DP, None),
        P(None, None, "z"),
        P(None, "z"),
        P("z", None),
        P(),
        P(),
        P(),
        P(None, "z"),
        P("z"),
        P("z", None),
        P(),
        P(),
        P(),
        P(),
        rows3,
        rows3,
    )
    out_specs = (
        rows3,
        rows3,
        rows3,
        P(None, None, "z"),
        P(None, "z"),
        P("z", None),
        P(),
        P(),
        P(),
        P(None, "z"),
        P("z"),
        P("z", None),
        P(),
        P(),
        P(),
        P(),
    )

    def run(*args):
        return per_device(side * side, *args)

    return jax.shard_map(run, mesh=cut, in_specs=in_specs, out_specs=out_specs, check_vma=False)
```

profile of v0, /device:TPU:0, one launch (start us, length us, event | category | flops | bytes accessed | tf_op | source)
XLA Modules:
  0.0 1139.8 jit_solution(14915674222163912071)
XLA Ops:
  16.3 2.8 broadcast_multiply_fusion
  19.1 74.0 %all-gather.8.cloned.1.call-done = bf16[2,1024,1024]{2,1,0:T(8,128)(2,1)} async-done(((bf16[2,256,1024]{2,1,0:T(8,128)(2,1)}), bf16[2,1024,1024]{2,1,0:T(8,128)(2,1)}) %all-gather.8.cloned.1.call-update) | async-done | bytes 4194320 | tf_op jit(solution)/shard_map/all_gather | solution.py:162
  93.1 6.1 add_bitcast_fusion
  102.7 7.3 select_reduce_fusion
  110.1 7.4 select_reduce_fusion.1
  117.5 8.8 fusion.1
  126.3 8.9 fusion
  135.3 8.4 fusion.69
  143.7 8.2 fusion.68
  154.1 3.6 all-to-all-start
  157.8 37.1 %all-gather = f32[4096]{0:T(1024)S(1)} all-gather(f32[1024]{0:T(1024)S(1)} %copy-done.31), channel_id=2, replica_groups=mesh['xb'=1,'x'=2,'yb'=1,'y'=2,'core'=2,'z'=4] {'z'}, dimensions={0}, use_global_device_ids=true | all-gather | bytes 20480 | tf_op jit(solution)/shard_map/all_gather | solution.py:166
  198.1 3.6 fusion.105
  203.3 39.1 %all-gather.12.cloned.1.call-done = bf16[4096,1024]{1,0:T(8,128)(2,1)} async-done(((bf16[128,1024]{1,0:T(8,128)(2,1)}), bf16[4096,1024]{1,0:T(8,128)(2,1)}) %all-gather.12.cloned.1.call-update) | async-done | bytes 8388624 | tf_op jit(solution)/shard_map/all_gather | solution.py:111
  242.4 27.7 %fusion.13 = (bf16[4,512,1024]{2,1,0:T(8,128)(2,1)}, f32[4,512,1024]{2,1,0:T(8,128)}, f32[4,1024,512]{1,2,0:T(8,128)}) fusion(f32[4,1024]{1,0:T(4,128)S(1)} %reshape.290, bf16[4,1024,1024]{2,1,0:T(8,128)(2,1)} %bitcast.330, f32[512,1024]{1,0:T(8,128)} %copy-done.11, f32[1024]{0:T(1024)S(1)} %copy-done.40, f32[1024]{0:T(1024)S(1)} %copy-done.30, ...), kind=kOutput, calls=%fused_computation.34 | convolution fusion | flops 4436000768 | bytes 31485952 | tf_op jit(solution)/shard_map/nd,zdf->znf/dot_general | solution.py:183
  270.1 51.6 %all-gather.14.cloned.1.call-done = bf16[4096,1024]{1,0:T(8,128)(2,1)} async-done(((bf16[128,1024]{1,0:T(8,128)(2,1)}), bf16[4096,1024]{1,0:T(8,128)(2,1)}) %all-gather.14.cloned.1.call-update) | async-done | bytes 8388624 | tf_op jit(solution)/shard_map/all_gather | solution.py:111
  321.8 10.0 fusion.106
  335.5 13.3 %convert_reduce_fusion = (f32[4,1024]{1,0:T(4,128)S(1)}, bf16[4,512,1024]{2,1,0:T(8,128)(2,1)}) fusion(f32[4,512,1024]{2,1,0:T(8,128)} %get-tuple-element.93, bf16[4,1024,1024]{2,1,0:T(8,128)(2,1)S(1)} %bitcast.335, f32[512,1024]{1,0:T(8,128)S(1)} %get-tuple-element.89, f32[4,1024,512]{1,2,0:T(8,128)} %get-tuple-element.127, f32[4,1024]{1,0:T(4,128)S(1)} %reshape.290), kind=kOutput, calls=%fused_computation.35 | convolution fusion | flops 4331139072 | bytes 31490048 | tf_op jit(solution)/shard_map/nd,zfd->znf/dot_general | solution.py:205
  348.8 10.0 convolution_convert_fusion.1
  358.9 10.7 convolution_convert_fusion
  369.6 11.8 %multiply_reduce_fusion.3 = (f32[1024]{0:T(1024)}, f32[512]{0:T(512)S(1)}, f32[512]{0:T(512)S(1)}, f32[1024]{0:T(1024)}, f32[512,1024]{1,0:T(8,128)S(1)}) fusion(f32[512,1024]{1,0:T(8,128)} %copy-done.11, f32[512]{0:T(512)S(1)} %add_rsqrt_fusion.1, f32[512]{0:T(512)S(1)} %broadcast_multiply_fusion.7, f32[1024]{0:T(1024)S(1)} %copy-done.30, ...), kind=kOutput, calls=%fused_computation.93 | convolution fusion | flops 4300207104 | bytes 18894848 | tf_op jit(solution)/shard_map/znf,zdf->nd/dot_general | solution.py:211
  385.3 3.7 copy.98
  389.0 4.3 all-to-all-start.1
  393.4 30.4 %all-to-all-done.1 = bf16[2,256,1024]{1,0,2:T(2,128)(2,1)} async-done(((bf16[2,256,1024]{1,0,2:T(2,128)(2,1)}), bf16[2,256,1024]{1,0,2:T(2,128)(2,1)}, u32[]{:S(2)}, u32[]{:S(2)}) %all-to-all-start.1) | async-done | bytes 1048608 | tf_op jit(solution)/shard_map/all_to_all | solution.py:224
  423.8 3.0 copy.143
  426.8 3.0 reshape.281
  429.8 10.6 fusion.70
  440.4 10.6 fusion.73
  455.6 11.9 %multiply_reduce_fusion = (f32[4,1024]{1,0:T(4,128)S(1)}, f32[4,1024,1024]{1,2,0:T(8,128)}) fusion(f32[4,1024,1024]{1,2,0:T(8,128)} %get-tuple-element.122, f32[4,1024]{1,0:T(4,128)S(1)} %log_add_fusion, pred[1024,1024]{0,1:T(8,128)(4,1)S(1)} %copy-done.4, bf16[2,4,1024,64]{2,3,1,0:T(8,128)(2,1)S(1)} %bitcast.300, bf16[2,4,1024,64]{2,3,1,0:T(8,128)(2,1)} %bitcast.304), kind=kOutput, calls=%fused_computation.1 | convolution fusion | flops 553644032 | bytes 35684352 | tf_op jit(solution)/shard_map/hqd,hkd->hqk/dot_general | solution.py:97
  467.4 12.5 %multiply_convert_fusion = bf16[4,1024,1024]{1,2,0:T(8,128)(2,1)S(1)} fusion(f32[4,1024,1024]{1,2,0:T(8,128)} %get-tuple-element.135, f32[4,1024,1024]{1,2,0:T(8,128)} %get-tuple-element.122, f32[4,1024]{1,0:T(4,128)S(1)} %get-tuple-element.134, f32[4,1024]{1,0:T(4,128)S(1)} %log_add_fusion, pred[1024,1024]{0,1:T(8,128)(4,1)S(1)} %copy-done.4), kind=kLoop, calls=%fused_computation | loop fusion | flops 20971520 | bytes 43024384 | tf_op jit(solution)/shard_map/convert_element_type | solution.py:99
  481.5 12.0 %multiply_reduce_fusion.1 = (f32[4,1024]{1,0:T(4,128)S(1)}, f32[4,1024,1024]{1,2,0:T(8,128)}) fusion(f32[4,1024,1024]{1,2,0:T(8,128)} %get-tuple-element.124, f32[4,1024]{1,0:T(4,128)S(1)} %log_add_fusion.1, pred[1024,1024]{0,1:T(8,128)(4,1)S(1)} %broadcast_compare_fusion.1, bf16[2,4,1024,64]{2,3,1,0:T(8,128)(2,1)S(1)} %bitcast.301, ...), kind=kOutput, calls=%fused_computation.4 | convolution fusion | flops 553644032 | bytes 35684352 | tf_op jit(solution)/shard_map/hqd,hkd->hqk/dot_general | solution.py:97
  493.5 12.2 %multiply_convert_fusion.1 = bf16[4,1024,1024]{1,2,0:T(8,128)(2,1)S(1)} fusion(f32[4,1024,1024]{1,2,0:T(8,128)} %get-tuple-element.137, f32[4,1024,1024]{1,2,0:T(8,128)} %get-tuple-element.124, f32[4,1024]{1,0:T(4,128)S(1)} %get-tuple-element.136, f32[4,1024]{1,0:T(4,128)S(1)} %log_add_fusion.1, pred[1024,1024]{0,1:T(8,128)(4,1)S(1)} %broadcast_compare_fusion.1), kind=kLoop, calls=%fused_computation.3 | loop fusion | flops 20971520 | bytes 43024384 | tf_op jit(solution)/shard_map/convert_element_type | solution.py:99
  512.8 6.1 convolution_bitcast_fusion.3
  526.3 7.9 fusion.57
  534.4 3.9 convolution_convert_fusion.2
  538.4 7.5 bitcast_convert_fusion
  546.6 112.0 %reduce-scatter.11.cloned.1.call-done = bf16[128,1024]{1,0:T(8,128)(2,1)} async-done(((bf16[4096,1024]{1,0:T(8,128)(2,1)}), bf16[128,1024]{1,0:T(8,128)(2,1)}) %reduce-scatter.11.cloned.1.call-update) | async-done | bytes 262160 | tf_op jit(solution)/shard_map/reduce_scatter | solution.py:117
  665.4 37.5 %psum.22 = f32[13312]{0:T(1024)S(1)} all-reduce(f32[13312]{0:T(1024)S(1)} %constant_dynamic-update-slice_fusion), channel_id=1, replica_groups=mesh['xb'=1,'x'=2,'yb'=1,'y'=2,'core'=2,'z'=4] {'xb','x','yb','y','core'..., use_global_device_ids=true, to_apply=%region_26.27 | all-reduce | flops 13312 | bytes 106496 | tf_op jit(solution)/shard_map/psum | solution.py:265
  704.2 13.4 %all-reduce.4.cloned.1.call-done = bf16[3,1024,256]{1,2,0:T(8,128)(2,1)} async-done(((bf16[3,1024,256]{1,2,0:T(8,128)(2,1)}), bf16[3,1024,256]{1,2,0:T(8,128)(2,1)}) %all-reduce.4.cloned.1.call-update) | async-done | bytes 1572880 | tf_op jit(solution)/shard_map/psum | solution.py:245
  717.5 3.1 copy.113
  720.6 136.1 %reduce-scatter.7.cloned.1.call-done = bf16[32,1024]{1,0:T(8,128)(2,1)} async-done(((bf16[1024,1024]{1,0:T(8,128)(2,1)}), bf16[32,1024]{1,0:T(8,128)(2,1)}) %reduce-scatter.7.cloned.1.call-update) | async-done | bytes 65552 | tf_op jit(solution)/shard_map/reduce_scatter | solution.py:117
  856.6 9.2 all_gather.33
  866.9 65.3 %reduce-scatter.5.cloned.1.call-done = bf16[2,256,1024]{2,1,0:T(8,128)(2,1)} async-done(((bf16[2,1024,1024]{2,1,0:T(8,128)(2,1)}), bf16[2,256,1024]{2,1,0:T(8,128)(2,1)}) %reduce-scatter.5.cloned.1.call-update) | async-done | bytes 1048592 | tf_op jit(solution)/shard_map/reduce_scatter | solution.py:243
  932.2 3.0 convert_add_fusion.2
  935.2 27.4 %all-gather.16.cloned.1.call-done = bf16[1024,1024]{1,0:T(8,128)(2,1)} async-done(((bf16[128,1024]{1,0:T(8,128)(2,1)}), bf16[1024,1024]{1,0:T(8,128)(2,1)}) %all-gather.16.cloned.1.call-update) | async-done | bytes 2097168 | tf_op jit(solution)/shard_map/all_gather | solution.py:120
  962.5 4.2 convert_element_type.168
  966.8 25.8 %all-gather.18.cloned.1.call-done = bf16[1024,1024]{1,0:T(8,128)(2,1)} async-done(((bf16[128,1024]{1,0:T(8,128)(2,1)}), bf16[1024,1024]{1,0:T(8,128)(2,1)}) %all-gather.18.cloned.1.call-update) | async-done | bytes 2097168 | tf_op jit(solution)/shard_map/all_gather | solution.py:120
  992.5 4.1 convert_element_type.170
  996.6 133.7 %all-reduce.6.cloned.1.call-done = f32[1024,288]{0,1:T(8,128)} async-done(((f32[1024,288]{0,1:T(8,128)}), f32[1024,288]{0,1:T(8,128)}) %all-reduce.6.cloned.1.call-update) | async-done | bytes 1179664 | tf_op jit(solution)/shard_map/psum | solution.py:266
  (189 shorter events, 59.9 us)
Async XLA Ops:
  7.2 85.9 %copy-start.37 = (f32[3,256]{1,0:T(4,128)S(1)}, f32[3,256]{1,0:T(4,128)}, u32[]{:S(2)}) copy-start(f32[3,256]{1,0:T(4,128)} %param.20) | copy-start | bytes 9220
  7.2 85.9 %all-gather.8.cloned.1.call-start = ((), (), s32[]{:S(2)}) async-start(), calls=%async_computation.6 | async-start | bytes 5242880 | tf_op jit(solution)/shard_map/all_gather | solution.py:162
  7.9 190.1 %all-gather.10.cloned.1.call-start = ((), (), s32[]{:S(2)}) async-start(), calls=%async_computation.7 | async-start | bytes 2162688 | tf_op jit(solution)/shard_map/all_gather | solution.py:111
  9.5 232.9 %all-gather.12.cloned.1.call-start = ((), (), s32[]{:S(2)}) async-start(), calls=%async_computation.8 | async-start | bytes 8650752 | tf_op jit(solution)/shard_map/all_gather | solution.py:111
  10.3 311.4 %all-gather.14.cloned.1.call-start = ((), (), s32[]{:S(2)}) async-start(), calls=%async_computation.9 | async-start | bytes 8650752 | tf_op jit(solution)/shard_map/all_gather | solution.py:111
  15.5 119.7 %copy-start.3 = (pred[1024,1024]{0,1:T(8,128)(4,1)}, pred[1024,1024]{0,1:T(8,128)(4,1)S(1)}, u32[]{:S(2)}) copy-start(pred[1024,1024]{0,1:T(8,128)(4,1)S(1)} %broadcast_compare_fusion) | copy-start | bytes 3145732
  19.1 82.4 %copy-start.14 = (f32[2,1024,64]{1,2,0:T(8,128)}, f32[2,1024,64]{1,2,0:T(8,128)S(1)}, u32[]{:S(2)}) copy-start(f32[2,1024,64]{1,2,0:T(8,128)S(1)} %get-tuple-element.110) | copy-start | bytes 1572868
  19.1 82.4 %copy-start.16 = (f32[2,1024,64]{1,2,0:T(8,128)}, f32[2,1024,64]{1,2,0:T(8,128)S(1)}, u32[]{:S(2)}) copy-start(f32[2,1024,64]{1,2,0:T(8,128)S(1)} %get-tuple-element.111) | copy-start | bytes 1572868
  102.7 7.3 copy-start.5
  102.7 7.3 copy-start.7
  110.1 25.2 %copy-start.24 = (f32[4,1024]{1,0:T(4,128)}, f32[4,1024]{1,0:T(4,128)S(1)}, u32[]{:S(2)}) copy-start(f32[4,1024]{1,0:T(4,128)S(1)} %get-tuple-element.121) | copy-start | bytes 49156
  126.3 8.9 copy-start.26
  126.3 8.9 copy-start.18
  151.9 5.9 copy-start.31
  154.1 44.0 %copy-start.38 = (f32[1024]{0:T(1024)S(1)}, f32[1024]{0:T(1024)}, u32[]{:S(2)}) copy-start(f32[1024]{0:T(1024)} %param.22) | copy-start | bytes 12292
  154.1 41.8 %all-to-all-start = ((bf16[2,1024,256]{2,0,1:T(2,128)(2,1)}), bf16[2,1024,256]{2,0,1:T(2,128)(2,1)S(1)}, u32[]{:S(2)}, u32[]{:S(2)}) async-start(bf16[2,1024,256]{2,0,1:T(2,128)(2,1)} %copy.94), calls=%async_computation | async-start | bytes 2097152 | tf_op jit(solution)/shard_map/all_to_all | solution.py:175
  157.8 388.3 %reduce-scatter.9.cloned.1.call-start = ((), (), s32[]{:S(2)}) async-start(), calls=%async_computation.13 | async-start | bytes 8650752 | tf_op jit(solution)/shard_map/reduce_scatter | solution.py:117
  198.1 44.3 %copy-start.30 = (f32[1024]{0:T(1024)S(1)}, f32[1024]{0:T(1024)}, u32[]{:S(2)}) copy-start(f32[1024]{0:T(1024)} %param.23) | copy-start | bytes 12292
  198.1 44.3 %copy-start.40 = (f32[1024]{0:T(1024)S(1)}, f32[1024]{0:T(1024)}, u32[]{:S(2)}) copy-start(f32[1024]{0:T(1024)} %param.24) | copy-start | bytes 12292
  242.4 79.4 %copy-start.39 = (f32[1024]{0:T(1024)S(1)}, f32[1024]{0:T(1024)}, u32[]{:S(2)}) copy-start(f32[1024]{0:T(1024)} %param.28) | copy-start | bytes 12292
  321.8 10.4 copy-start.28
  321.8 10.4 copy-start.35
  321.8 10.4 copy-start.36
  331.8 3.7 slice-start
  332.2 3.3 slice-start.1
  335.5 13.3 %copy-start.22 = (f32[512,1024]{1,0:T(8,128)}, f32[512,1024]{1,0:T(8,128)S(1)}, u32[]{:S(2)}) copy-start(f32[512,1024]{1,0:T(8,128)S(1)} %get-tuple-element.89) | copy-start | bytes 6291460
  335.5 13.3 %copy-start.12 = (f32[512,1024]{1,0:T(8,128)S(1)}, f32[512,1024]{1,0:T(8,128)}, u32[]{:S(2)}) copy-start(f32[512,1024]{1,0:T(8,128)} %copy-done.11) | copy-start | bytes 6291460
  358.8 299.8 %reduce-scatter.11.cloned.1.call-start = ((), (), s32[]{:S(2)}) async-start(), calls=%async_computation.15 | async-start | bytes 8650752 | tf_op jit(solution)/shard_map/reduce_scatter | solution.py:117
  369.6 11.8 %copy-start.13 = (f32[512,1024]{1,0:T(8,128)S(1)}, f32[512,1024]{1,0:T(8,128)}, u32[]{:S(2)}) copy-start(f32[512,1024]{1,0:T(8,128)} %copy-done.11) | copy-start | bytes 6291460
  382.1 3.2 copy-start.9
  383.0 10.4 copy-start.25
  383.0 10.4 copy-start.27
  385.3 44.5 %copy-start.4 = (pred[1024,1024]{0,1:T(8,128)(4,1)S(1)}, pred[1024,1024]{0,1:T(8,128)(4,1)}, u32[]{:S(2)}) copy-start(pred[1024,1024]{0,1:T(8,128)(4,1)} %copy-done.3) | copy-start | bytes 3145732
  389.0 34.8 %all-to-all-start.1 = ((bf16[2,256,1024]{1,0,2:T(2,128)(2,1)}), bf16[2,256,1024]{1,0,2:T(2,128)(2,1)}, u32[]{:S(2)}, u32[]{:S(2)}) async-start(bf16[2,256,1024]{1,0,2:T(2,128)(2,1)} %copy.98), calls=%async_computation.1 | async-start | bytes 2097152 | tf_op jit(solution)/shard_map/all_to_all | solution.py:224
  393.3 324.2 %all-reduce.4.cloned.1.call-start = ((), (), s32[]{:S(2)}) async-start(), calls=%async_computation.11 | async-start | bytes 3145728 | tf_op jit(solution)/shard_map/psum | solution.py:245
  467.4 12.5 %copy-start.8 = (bf16[2,4,1024,64]{2,3,1,0:T(8,128)(2,1)S(1)}, bf16[2,4,1024,64]{2,3,1,0:T(8,128)(2,1)}, u32[]{:S(2)}) copy-start(bf16[2,4,1024,64]{2,3,1,0:T(8,128)(2,1)} %copy-done.7) | copy-start | bytes 3145732
  505.7 3.2 copy-start.2
  526.3 8.0 copy-start.10
  534.3 4.1 copy-start.21
  534.3 322.3 %reduce-scatter.7.cloned.1.call-start = ((), (), s32[]{:S(2)}) async-start(), calls=%async_computation.12 | async-start | bytes 2162688 | tf_op jit(solution)/shard_map/reduce_scatter | solution.py:117
  538.3 393.8 %reduce-scatter.5.cloned.1.call-start = ((), (), s32[]{:S(2)}) async-start(), calls=%async_computation.10 | async-start | bytes 5242880 | tf_op jit(solution)/shard_map/reduce_scatter | solution.py:243
  545.9 112.8 %copy-start.20 = (bf16[512,1024]{1,0:T(8,128)(2,1)S(1)}, bf16[512,1024]{1,0:T(8,128)(2,1)}, u32[]{:S(2)}) copy-start(bf16[512,1024]{1,0:T(8,128)(2,1)} %get-tuple-element.96) | copy-start | bytes 3145732
  545.9 115.1 %copy-start.33 = (f32[1024]{0:T(1024)S(1)}, f32[1024]{0:T(1024)}, u32[]{:S(2)}) copy-start(f32[1024]{0:T(1024)} %get-tuple-element.82) | copy-start | bytes 12292
  545.9 115.1 %copy-start.32 = (f32[1024]{0:T(1024)S(1)}, f32[1024]{0:T(1024)}, u32[]{:S(2)}) copy-start(f32[1024]{0:T(1024)} %get-tuple-element.87) | copy-start | bytes 12292
  546.0 416.6 %all-gather.16.cloned.1.call-start = ((), (), s32[]{:S(2)}) async-start(), calls=%async_computation.14 | async-start | bytes 2359296 | tf_op jit(solution)/shard_map/all_gather | solution.py:120
  546.6 446.0 %all-gather.18.cloned.1.call-start = ((), (), s32[]{:S(2)}) async-start(), calls=%async_computation.16 | async-start | bytes 2359296 | tf_op jit(solution)/shard_map/all_gather | solution.py:120
  658.7 471.6 %all-reduce.6.cloned.1.call-start = ((), (), s32[]{:S(2)}) async-start(), calls=%async_computation.17 | async-start | bytes 2359296 | tf_op jit(solution)/shard_map/psum | solution.py:266
  962.5 170.2 %copy-start.1 = (bf16[1024,1024]{1,0:T(8,128)(2,1)S(1)}, bf16[1024,1024]{1,0:T(8,128)(2,1)}, u32[]{:S(2)}) copy-start(bf16[1024,1024]{1,0:T(8,128)(2,1)} %param.25) | copy-start | bytes 6291460
  (9 other events, 13.6 us)
Sparse Core Ops, SparseCore 0:
  9.6 83.4 all-gather.7
  96.5 54.8 all-gather.9
  154.9 87.4 all-gather.11
  245.7 76.0 all-gather.13
  358.9 151.9 reduce-scatter.8
  513.1 145.5 reduce-scatter.10
  662.5 55.0 all-reduce.3
  720.5 136.1 reduce-scatter.6
  859.5 72.6 reduce-scatter.4
  934.1 28.4 all-gather.15
  964.6 27.8 all-gather.17
  999.2 131.0 all-reduce.5
where the time goes:
time: 1150 us; the launch traced here: 1140 us
  waiting for transfers between devices  710 us (62%)
  matrix products  208 us (18%)
  blocking collectives  83.7 us (7%)
  other arithmetic  73.9 us (6%)
  local copies, waits for them, and re-layouts  40.8 us (4%)
  between operations  15.2 us (1%)
    reduce_scatter x3, waiting for transfers between devices, reduce_all(): lax.psum_scatter(partial.reshape(rows, partial.shape[2]), ('z',) + CELL,...  248 us
    psum x1, waiting for transfers between devices, per_device(): proj_grad = lax.psum(proj_grad, ALL)  134 us
    all_gather x3, waiting for transfers between devices, gather_all(): whole = lax.all_gather(piece_of(shard), ('z',) + CELL, axis=0, tiled=True)  90.7 us
    all_gather x1, waiting for transfers between devices, per_device(): whole_tokens = lax.all_gather(tokens, 'z', axis=1, tiled=True)  74 us
    reduce_scatter x1, waiting for transfers between devices, per_device(): lax.psum_scatter(input_back, 'z', scatter_dimension=1, tiled=True)  65.3 us
    all_gather x2, waiting for transfers between devices, reduce_all(): return lax.all_gather(piece, CELL, axis=0, tiled=True)  53.1 us
    psum x1, blocking collectives, per_device(): small = lax.psum(small, ALL)  37.5 us
    all_gather x1, blocking collectives, per_device(): full_up_bias = lax.all_gather(up_bias, 'z', axis=0, tiled=False)  37.1 us
  transfers between devices with their start and end apart: 14, of which 11 were waited for; matrix products, arithmetic and copies ran while one was open for 24% of the time, Pallas kernels for 0%

commit v1 on v0

--- a/solution.py
+++ b/solution.py
@@ -263,7 +263,7 @@
         ]
     )
     small = lax.psum(small, ALL)
-    proj_grad = lax.psum(proj_grad, ALL)
+    proj_grad = jnp.sum(lax.all_gather(proj_grad, ALL), axis=0)
     base = 6 * model_width
     vec = [small[i * model_width : (i + 1) * model_width] for i in range(6)]
     up_bias_grad = lax.dynamic_slice(small, (base + zi * units_here,), (units_here,))

time: 1150 us -> 1270 us (1.10)
  waiting for transfers between devices: 710 us -> 800 us
  local copies, waits for them, and re-layouts: 40.8 us -> 65.5 us
    all_gather x0 -> x1, waiting for transfers between devices: none -> 216 us  [per_device(): proj_grad = jnp.sum(lax.all_gather(proj_grad, ALL), axis=0)]
    psum x1 -> x0, waiting for transfers between devices: 134 us -> none  [per_device(): proj_grad = lax.psum(proj_grad, ALL)]
    unnamed x98 -> x110, local copies, waits for them, and re-layouts: 12.6 us -> 40.6 us
  transfers between devices with their start and end apart: 14 -> 14, of which waited for: 11 -> 11; matrix products, arithmetic and copies ran while one was open for 24% -> 22% of each run, Pallas kernels for 0% -> 0%
where the time goes in v1:
time: 1270 us; the launch traced here: 1260 us
  waiting for transfers between devices  800 us (63%)
  matrix products  201 us (16%)
  other arithmetic  86.4 us (7%)
  blocking collectives  83.7 us (7%)
  local copies, waits for them, and re-layouts  65.5 us (5%)
  between operations  15.6 us (1%)
    reduce_scatter x3, waiting for transfers between devices, reduce_all(): lax.psum_scatter(partial.reshape(rows, partial.shape[2]), ('z',) + CELL,...  253 us
    all_gather x1, waiting for transfers between devices, per_device(): proj_grad = jnp.sum(lax.all_gather(proj_grad, ALL), axis=0)  216 us
    all_gather x3, waiting for transfers between devices, gather_all(): whole = lax.all_gather(piece_of(shard), ('z',) + CELL, axis=0, tiled=True)  93.7 us
    all_gather x1, waiting for transfers between devices, per_device(): whole_tokens = lax.all_gather(tokens, 'z', axis=1, tiled=True)  74 us
    reduce_scatter x1, waiting for transfers between devices, per_device(): lax.psum_scatter(input_back, 'z', scatter_dimension=1, tiled=True)  65.3 us
    all_gather x2, waiting for transfers between devices, reduce_all(): return lax.all_gather(piece, CELL, axis=0, tiled=True)  53.3 us
    unnamed x110, local copies, waits for them, and re-layouts  40.6 us
    psum x1, blocking collectives, per_device(): small = lax.psum(small, ALL)  37.5 us
  transfers between devices with their start and end apart: 14, of which 11 were waited for; matrix products, arithmetic and copies ran while one was open for 22% of the time, Pallas kernels for 0%

profile of v1, /device:TPU:0, one launch (start us, length us, event | category | flops | bytes accessed | tf_op | source)
XLA Modules:
  0.0 1260.5 jit_solution(3302357586889776213)
XLA Ops:
  15.0 2.8 broadcast_multiply_fusion
  19.1 74.0 %all-gather.10.cloned.1.call-done = bf16[2,1024,1024]{2,1,0:T(8,128)(2,1)} async-done(((bf16[2,256,1024]{2,1,0:T(8,128)(2,1)}), bf16[2,1024,1024]{2,1,0:T(8,128)(2,1)}) %all-gather.10.cloned.1.call-update) | async-done | bytes 4194320 | tf_op jit(solution)/shard_map/all_gather | solution.py:162
  93.1 6.1 add_bitcast_fusion
  102.7 7.3 select_reduce_fusion.1
  110.0 7.5 select_reduce_fusion
  117.6 8.8 fusion
  126.4 8.9 fusion.1
  135.3 8.4 fusion.68
  143.8 8.3 fusion.69
  154.2 3.6 all-to-all-start
  157.9 37.0 %all-gather = f32[4096]{0:T(1024)S(1)} all-gather(f32[1024]{0:T(1024)S(1)} %copy-done.35), channel_id=2, replica_groups=mesh['xb'=1,'x'=2,'yb'=1,'y'=2,'core'=2,'z'=4] {'z'}, dimensions={0}, use_global_device_ids=true | all-gather | bytes 20480 | tf_op jit(solution)/shard_map/all_gather | solution.py:166
  197.2 3.6 fusion.105
  201.1 41.3 %all-gather.14.cloned.1.call-done = bf16[4096,1024]{1,0:T(8,128)(2,1)} async-done(((bf16[128,1024]{1,0:T(8,128)(2,1)}), bf16[4096,1024]{1,0:T(8,128)(2,1)}) %all-gather.14.cloned.1.call-update) | async-done | bytes 8388624 | tf_op jit(solution)/shard_map/all_gather | solution.py:111
  242.5 27.0 %fusion.13 = (bf16[4,512,1024]{2,1,0:T(8,128)(2,1)}, f32[4,512,1024]{2,1,0:T(8,128)}, f32[4,1024,512]{1,2,0:T(8,128)}) fusion(f32[4,1024]{1,0:T(4,128)S(1)} %reshape.290, bf16[4,1024,1024]{2,1,0:T(8,128)(2,1)} %bitcast.337, f32[512,1024]{1,0:T(8,128)S(1)} %get-tuple-element.126, f32[1024]{0:T(1024)S(1)} %copy-done.45, f32[1024]{0:T(1024)S(1)} %copy-done.34, ...), kind=kOutput, calls=%fused_computation.35 | convolution fusion | flops 4436000768 | bytes 31485952 | tf_op jit(solution)/shard_map/nd,zdf->znf/dot_general | solution.py:183
  269.5 52.4 %all-gather.16.cloned.1.call-done = bf16[4096,1024]{1,0:T(8,128)(2,1)} async-done(((bf16[128,1024]{1,0:T(8,128)(2,1)}), bf16[4096,1024]{1,0:T(8,128)(2,1)}) %all-gather.16.cloned.1.call-update) | async-done | bytes 8388624 | tf_op jit(solution)/shard_map/all_gather | solution.py:111
  321.9 8.6 fusion.106
  334.7 13.0 %convert_reduce_fusion = (f32[4,1024]{1,0:T(4,128)S(1)}, bf16[4,512,1024]{2,1,0:T(8,128)(2,1)}) fusion(f32[4,512,1024]{2,1,0:T(8,128)} %get-tuple-element.93, bf16[4,1024,1024]{2,1,0:T(8,128)(2,1)S(1)} %bitcast.342, f32[512,1024]{1,0:T(8,128)S(1)} %get-tuple-element.89, f32[4,1024,512]{1,2,0:T(8,128)} %get-tuple-element.127, f32[4,1024]{1,0:T(4,128)S(1)} %reshape.290), kind=kOutput, calls=%fused_computation.36 | convolution fusion | flops 4331139072 | bytes 31490048 | tf_op jit(solution)/shard_map/nd,zfd->znf/dot_general | solution.py:205
  347.7 10.0 convolution_convert_fusion.1
  358.0 10.7 convolution_convert_fusion
  368.7 11.1 multiply_reduce_fusion.3
  384.5 3.7 copy.98
  388.3 3.5 all-to-all-start.1
  392.3 30.2 %all-to-all-done.1 = bf16[2,256,1024]{1,0,2:T(2,128)(2,1)S(1)} async-done(((bf16[2,256,1024]{1,0,2:T(2,128)(2,1)}), bf16[2,256,1024]{1,0,2:T(2,128)(2,1)S(1)}, u32[]{:S(2)}, u32[]{:S(2)}) %all-to-all-start.1) | async-done | bytes 1048608 | tf_op jit(solution)/shard_map/all_to_all | solution.py:224
  426.1 12.3 multiply_reduce_fusion.1
  438.5 12.3 multiply_convert_fusion.1
  453.5 12.0 multiply_reduce_fusion
  465.5 15.8 %multiply_convert_fusion = bf16[4,1024,1024]{1,2,0:T(8,128)(2,1)} fusion(f32[4,1024,1024]{1,2,0:T(8,128)} %get-tuple-element.135, f32[4,1024,1024]{1,2,0:T(8,128)} %get-tuple-element.122, f32[4,1024]{1,0:T(4,128)S(1)} %get-tuple-element.134, f32[4,1024]{1,0:T(4,128)S(1)} %log_add_fusion, pred[1024,1024]{0,1:T(8,128)(4,1)S(1)} %copy-done.4), kind=kLoop, calls=%fused_computation.1 | loop fusion | flops 20971520 | bytes 43024384 | tf_op jit(solution)/shard_map/convert_element_type | solution.py:99
  481.3 6.1 convolution_bitcast_fusion.2
  502.1 8.8 fusion.73
  510.9 8.2 fusion.70
  520.7 7.7 fusion.57
  528.5 3.8 convolution_convert_fusion.2
  532.4 7.6 bitcast_convert_fusion
  540.7 116.7 %reduce-scatter.11.cloned.1.call-done = bf16[128,1024]{1,0:T(8,128)(2,1)} async-done(((bf16[4096,1024]{1,0:T(8,128)(2,1)}), bf16[128,1024]{1,0:T(8,128)(2,1)}) %reduce-scatter.11.cloned.1.call-update) | async-done | bytes 262160 | tf_op jit(solution)/shard_map/reduce_scatter | solution.py:117
  664.1 37.5 %psum.15 = f32[13312]{0:T(1024)S(1)} all-reduce(f32[13312]{0:T(1024)S(1)} %constant_dynamic-update-slice_fusion), channel_id=1, replica_groups=mesh['xb'=1,'x'=2,'yb'=1,'y'=2,'core'=2,'z'=4] {'xb','x','yb','y','core'..., use_global_device_ids=true, to_apply=%region_26.27 | all-reduce | flops 13312 | bytes 106496 | tf_op jit(solution)/shard_map/psum | solution.py:265
  703.0 13.3 %all-reduce.3.cloned.1.call-done = bf16[3,1024,256]{1,2,0:T(8,128)(2,1)} async-done(((bf16[3,1024,256]{1,2,0:T(8,128)(2,1)}), bf16[3,1024,256]{1,2,0:T(8,128)(2,1)}) %all-reduce.3.cloned.1.call-update) | async-done | bytes 1572880 | tf_op jit(solution)/shard_map/psum | solution.py:245
  716.3 3.1 copy.113
  719.3 136.0 %reduce-scatter.7.cloned.1.call-done = bf16[32,1024]{1,0:T(8,128)(2,1)} async-done(((bf16[1024,1024]{1,0:T(8,128)(2,1)}), bf16[32,1024]{1,0:T(8,128)(2,1)}) %reduce-scatter.7.cloned.1.call-update) | async-done | bytes 65552 | tf_op jit(solution)/shard_map/reduce_scatter | solution.py:117
  855.3 9.2 all_gather.39
  865.6 65.3 %reduce-scatter.5.cloned.1.call-done = bf16[2,256,1024]{2,1,0:T(8,128)(2,1)} async-done(((bf16[2,1024,1024]{2,1,0:T(8,128)(2,1)}), bf16[2,256,1024]{2,1,0:T(8,128)(2,1)}) %reduce-scatter.5.cloned.1.call-update) | async-done | bytes 1048592 | tf_op jit(solution)/shard_map/reduce_scatter | solution.py:243
  930.8 3.0 convert_add_fusion.2
  933.8 27.4 %all-gather.18.cloned.1.call-done = bf16[1024,1024]{1,0:T(8,128)(2,1)} async-done(((bf16[128,1024]{1,0:T(8,128)(2,1)}), bf16[1024,1024]{1,0:T(8,128)(2,1)}) %all-gather.18.cloned.1.call-update) | async-done | bytes 2097168 | tf_op jit(solution)/shard_map/all_gather | solution.py:120
  961.2 4.1 convert_element_type.168
  965.3 25.9 %all-gather.20.cloned.1.call-done = bf16[1024,1024]{1,0:T(8,128)(2,1)} async-done(((bf16[128,1024]{1,0:T(8,128)(2,1)}), bf16[1024,1024]{1,0:T(8,128)(2,1)}) %all-gather.20.cloned.1.call-update) | async-done | bytes 2097168 | tf_op jit(solution)/shard_map/all_gather | solution.py:120
  991.2 4.1 convert_element_type.170
  995.3 216.2 %all-gather.22.cloned.1.call-done = f32[32768,288]{0,1:T(8,128)} async-done(((f32[1024,288]{0,1:T(8,128)}), f32[32768,288]{0,1:T(8,128)}) %all-gather.22.cloned.1.call-update) | async-done | bytes 37748752 | tf_op jit(solution)/shard_map/all_gather | solution.py:266
  1211.4 32.3 %copy.138 = f32[36,8,32,1024]{3,2,1,0:T(8,128)S(1)} copy(f32[36,8,32,1024]{3,1,2,0:T(8,128)} %bitcast.296) | data formatting | bytes 75497472
  1243.8 9.5 bitcast_reduce_fusion
  (202 shorter events, 59.1 us)
Async XLA Ops:
  7.2 85.9 %copy-start.42 = (f32[3,256]{1,0:T(4,128)S(1)}, f32[3,256]{1,0:T(4,128)}, u32[]{:S(2)}) copy-start(f32[3,256]{1,0:T(4,128)} %param.20) | copy-start | bytes 9220
  7.2 85.9 %all-gather.10.cloned.1.call-start = ((), (), s32[]{:S(2)}) async-start(), calls=%async_computation.6 | async-start | bytes 5242880 | tf_op jit(solution)/shard_map/all_gather | solution.py:162
  7.9 189.3 %all-gather.12.cloned.1.call-start = ((), (), s32[]{:S(2)}) async-start(), calls=%async_computation.7 | async-start | bytes 2162688 | tf_op jit(solution)/shard_map/all_gather | solution.py:111
  9.5 232.9 %all-gather.14.cloned.1.call-start = ((), (), s32[]{:S(2)}) async-start(), calls=%async_computation.8 | async-start | bytes 8650752 | tf_op jit(solution)/shard_map/all_gather | solution.py:111
  10.3 311.6 %all-gather.16.cloned.1.call-start = ((), (), s32[]{:S(2)}) async-start(), calls=%async_computation.9 | async-start | bytes 8650752 | tf_op jit(solution)/shard_map/all_gather | solution.py:111
  17.8 83.6 %copy-start.14 = (f32[2,1024,64]{1,2,0:T(8,128)}, f32[2,1024,64]{1,2,0:T(8,128)S(1)}, u32[]{:S(2)}) copy-start(f32[2,1024,64]{1,2,0:T(8,128)S(1)} %get-tuple-element.110) | copy-start | bytes 1572868
  17.8 83.7 %copy-start.16 = (f32[2,1024,64]{1,2,0:T(8,128)}, f32[2,1024,64]{1,2,0:T(8,128)S(1)}, u32[]{:S(2)}) copy-start(f32[2,1024,64]{1,2,0:T(8,128)S(1)} %get-tuple-element.111) | copy-start | bytes 1572868
  18.5 116.8 %copy-start.5 = (pred[1024,1024]{0,1:T(8,128)(4,1)}, pred[1024,1024]{0,1:T(8,128)(4,1)S(1)}, u32[]{:S(2)}) copy-start(pred[1024,1024]{0,1:T(8,128)(4,1)S(1)} %broadcast_compare_fusion.1) | copy-start | bytes 3145732
  19.1 124.6 %copy-start.3 = (pred[1024,1024]{0,1:T(8,128)(4,1)}, pred[1024,1024]{0,1:T(8,128)(4,1)S(1)}, u32[]{:S(2)}) copy-start(pred[1024,1024]{0,1:T(8,128)(4,1)S(1)} %broadcast_compare_fusion) | copy-start | bytes 3145732
  102.7 7.3 copy-start.7
  102.7 7.3 copy-start.9
  110.0 25.3 %copy-start.28 = (f32[4,1024]{1,0:T(4,128)}, f32[4,1024]{1,0:T(4,128)S(1)}, u32[]{:S(2)}) copy-start(f32[4,1024]{1,0:T(4,128)S(1)} %get-tuple-element.123) | copy-start | bytes 49156
  126.4 8.9 copy-start.30
  126.4 8.9 copy-start.18
  152.0 5.9 copy-start.35
  152.1 42.9 %copy-start.27 = (bf16[2,256,288]{1,2,0:T(8,128)(2,1)S(1)}, bf16[2,256,288]{1,2,0:T(8,128)(2,1)}, u32[]{:S(2)}) copy-start(bf16[2,256,288]{1,2,0:T(8,128)(2,1)} %param.33) | copy-start | bytes 884740
  154.2 43.0 %copy-start.43 = (f32[1024]{0:T(1024)S(1)}, f32[1024]{0:T(1024)}, u32[]{:S(2)}) copy-start(f32[1024]{0:T(1024)} %param.22) | copy-start | bytes 12292
  154.2 40.8 %all-to-all-start = ((bf16[2,1024,256]{2,0,1:T(2,128)(2,1)}), bf16[2,1024,256]{2,0,1:T(2,128)(2,1)S(1)}, u32[]{:S(2)}, u32[]{:S(2)}) async-start(bf16[2,1024,256]{2,0,1:T(2,128)(2,1)} %copy.94), calls=%async_computation | async-start | bytes 2097152 | tf_op jit(solution)/shard_map/all_to_all | solution.py:175
  157.9 382.3 %reduce-scatter.9.cloned.1.call-start = ((), (), s32[]{:S(2)}) async-start(), calls=%async_computation.13 | async-start | bytes 8650752 | tf_op jit(solution)/shard_map/reduce_scatter | solution.py:117
  197.2 45.2 %copy-start.34 = (f32[1024]{0:T(1024)S(1)}, f32[1024]{0:T(1024)}, u32[]{:S(2)}) copy-start(f32[1024]{0:T(1024)} %param.23) | copy-start | bytes 12292
  197.2 45.2 %copy-start.45 = (f32[1024]{0:T(1024)S(1)}, f32[1024]{0:T(1024)}, u32[]{:S(2)}) copy-start(f32[1024]{0:T(1024)} %param.24) | copy-start | bytes 12292
  200.8 167.9 %copy-start.13 = (f32[512,1024]{1,0:T(8,128)}, f32[512,1024]{1,0:T(8,128)S(1)}, u32[]{:S(2)}) copy-start(f32[512,1024]{1,0:T(8,128)S(1)} %get-tuple-element.126) | copy-start | bytes 6291460
  242.5 79.5 %copy-start.44 = (f32[1024]{0:T(1024)S(1)}, f32[1024]{0:T(1024)}, u32[]{:S(2)}) copy-start(f32[1024]{0:T(1024)} %param.28) | copy-start | bytes 12292
  321.9 9.0 copy-start.32
  321.9 9.0 copy-start.40
  321.9 9.0 copy-start.41
  334.7 13.0 %copy-start.24 = (f32[512,1024]{1,0:T(8,128)}, f32[512,1024]{1,0:T(8,128)S(1)}, u32[]{:S(2)}) copy-start(f32[512,1024]{1,0:T(8,128)S(1)} %get-tuple-element.89) | copy-start | bytes 6291460
  334.7 13.0 %copy-start.46 = (f32[1024]{0:T(1024)S(1)}, f32[1024]{0:T(1024)}, u32[]{:S(2)}) copy-start(f32[1024]{0:T(1024)} %param.24) | copy-start | bytes 12292
  357.7 299.7 %reduce-scatter.11.cloned.1.call-start = ((), (), s32[]{:S(2)}) async-start(), calls=%async_computation.15 | async-start | bytes 8650752 | tf_op jit(solution)/shard_map/reduce_scatter | solution.py:117
  382.2 10.0 copy-start.29
  382.2 10.0 copy-start.31
  384.5 41.6 %copy-start.6 = (pred[1024,1024]{0,1:T(8,128)(4,1)S(1)}, pred[1024,1024]{0,1:T(8,128)(4,1)}, u32[]{:S(2)}) copy-start(pred[1024,1024]{0,1:T(8,128)(4,1)} %copy-done.5) | copy-start | bytes 3145732
  388.3 34.2 %all-to-all-start.1 = ((bf16[2,256,1024]{1,0,2:T(2,128)(2,1)}), bf16[2,256,1024]{1,0,2:T(2,128)(2,1)S(1)}, u32[]{:S(2)}, u32[]{:S(2)}) async-start(bf16[2,256,1024]{1,0,2:T(2,128)(2,1)} %copy.98), calls=%async_computation.1 | async-start | bytes 2097152 | tf_op jit(solution)/shard_map/all_to_all | solution.py:224
  391.8 324.5 %all-reduce.3.cloned.1.call-start = ((), (), s32[]{:S(2)}) async-start(), calls=%async_computation.11 | async-start | bytes 3145728 | tf_op jit(solution)/shard_map/psum | solution.py:245
  426.1 12.4 copy-start.19
  438.5 12.3 copy-start.10
  510.9 8.2 copy-start.26
  520.7 7.8 copy-start.12
  528.5 326.8 %reduce-scatter.7.cloned.1.call-start = ((), (), s32[]{:S(2)}) async-start(), calls=%async_computation.12 | async-start | bytes 2162688 | tf_op jit(solution)/shard_map/reduce_scatter | solution.py:117
  532.4 398.5 %reduce-scatter.5.cloned.1.call-start = ((), (), s32[]{:S(2)}) async-start(), calls=%async_computation.10 | async-start | bytes 5242880 | tf_op jit(solution)/shard_map/reduce_scatter | solution.py:243
  540.0 117.4 %copy-start.22 = (bf16[512,1024]{1,0:T(8,128)(2,1)S(1)}, bf16[512,1024]{1,0:T(8,128)(2,1)}, u32[]{:S(2)}) copy-start(bf16[512,1024]{1,0:T(8,128)(2,1)} %get-tuple-element.96) | copy-start | bytes 3145732
  540.1 121.3 %copy-start.38 = (f32[1024]{0:T(1024)S(1)}, f32[1024]{0:T(1024)}, u32[]{:S(2)}) copy-start(f32[1024]{0:T(1024)} %get-tuple-element.82) | copy-start | bytes 12292
  540.1 121.2 %copy-start.37 = (f32[1024]{0:T(1024)S(1)}, f32[1024]{0:T(1024)}, u32[]{:S(2)}) copy-start(f32[1024]{0:T(1024)} %get-tuple-element.87) | copy-start | bytes 12292
  540.1 121.3 %copy-start.36 = (f32[1024]{0:T(1024)S(1)}, f32[1024]{0:T(1024)}, u32[]{:S(2)}) copy-start(f32[1024]{0:T(1024)} %get-tuple-element.80) | copy-start | bytes 12292
  540.1 421.1 %all-gather.18.cloned.1.call-start = ((), (), s32[]{:S(2)}) async-start(), calls=%async_computation.14 | async-start | bytes 2359296 | tf_op jit(solution)/shard_map/all_gather | solution.py:120
  540.7 450.5 %all-gather.20.cloned.1.call-start = ((), (), s32[]{:S(2)}) async-start(), calls=%async_computation.16 | async-start | bytes 2359296 | tf_op jit(solution)/shard_map/all_gather | solution.py:120
  657.4 554.0 %all-gather.22.cloned.1.call-start = ((), (), s32[]{:S(2)}) async-start(), calls=%async_computation.17 | async-start | bytes 38928384 | tf_op jit(solution)/shard_map/all_gather | solution.py:266
  1243.7 9.5 copy-start.1
  (15 other events, 37.4 us)
Sparse Core Ops, SparseCore 0:
  9.6 83.4 all-gather.9
  96.5 54.8 all-gather.11
  154.9 87.4 all-gather.13
  245.7 76.1 all-gather.15
  357.8 151.8 reduce-scatter.8
  511.8 145.5 reduce-scatter.10
  661.2 54.9 all-reduce.2
  719.2 136.0 reduce-scatter.6
  858.2 72.6 reduce-scatter.4
  932.7 28.4 all-gather.17
  963.3 27.8 all-gather.19
  995.1 216.2 all-gather.21
